TPU v7x, 32 devices: a whole 2x2x4 slice. The times are simulated.
32 devices in a mesh: section: 2 (over core), fsdp: 4 (over z), dp: 4 (over y, x).
Axes of the slice: x: 2, y: 2, z: 4, core: 2. Of those that a mesh axis runs over, the one named last changes fastest.
Arguments:
- tokens: bfloat16 [1, 16, 128, 1024], P(None, ('fsdp', 'dp')), may hold values from -6 to 6
- segments: int32 [1, 16, 128], P(None, ('fsdp', 'dp')), may hold values from 0 to 3, never falling along the last dimension, each value on 1 to 64 neighbouring positions
- cotangent: float32 [1, 16, 128, 1024], P(None, ('fsdp', 'dp')), may hold values from -6 to 6
- norm_gains: bfloat16 [2, 2, 1024], P('section', None, 'fsdp'), may hold values from 0.5 to 1.5
- proj_weight: bfloat16 [2, 1024, 3072], P('section', 'fsdp'), may hold values from -0.1875 to 0.1875
- rate_weight: bfloat16 [2, 1024, 8], P('section', 'fsdp'), may hold values from -0.1875 to 0.1875
- out_weight: bfloat16 [2, 1024, 1024], P('section', 'fsdp'), may hold values from -0.375 to 0.375
- up_weight: bfloat16 [2, 1024, 5632], P('section', 'fsdp'), may hold values from -0.1875 to 0.1875
- down_weight: bfloat16 [2, 1024, 2816], P('section', 'fsdp'), may hold values from -0.21875 to 0.21875
- conv_kernels: float32 [2, 4, 2048], P('section'), may hold values from -3 to 3
- head_params: float32 [2, 2, 4], P('section'), may hold values from -2.5 to 0.5
- out_gain: float32 [2, 256], P('section'), may hold values from 0.5 to 1.5
Outputs:
- section_output: bfloat16 [2, 1, 16, 128, 1024], P('section', None, ('fsdp', 'dp'))
- input_grad: float32 [2, 1, 16, 128, 1024], P('section', None, ('fsdp', 'dp'))
- gains_grad: float32 [2, 2, 1024], P('section', None, 'fsdp')
- proj_grad: float32 [2, 1024, 3072], P('section', 'fsdp')
- rate_grad: float32 [2, 1024, 8], P('section', 'fsdp')
- out_grad: float32 [2, 1024, 1024], P('section', 'fsdp')
- up_grad: float32 [2, 1024, 5632], P('section', 'fsdp')
- down_grad: float32 [2, 1024, 2816], P('section', 'fsdp')
- kernel_grad: float32 [2, 4, 2048], P('section')
- head_grad: float32 [2, 2, 4], P('section')
- out_gain_grad: float32 [2, 256], P('section')
Inputs may be any that keep to these rules, and one draw needn't show every extreme that they name: `segments`: within each sequence the numbers never fall, every one of 0 .. 3 occurs, and each document holds 1 to 64 positions, one exactly 64.
All inputs are finite; a program needn't handle non-finite values.
Results may differ from a plain program's by a relative error of at most 0.034.
Values may be sent and summed in bfloat16 or wider, within the bound.
A program may use at most 256 MiB of HBM per device.

v0:
```python
from functools import partial
import jax
import jax.numpy as jnp
from jax import lax
from jax.sharding import PartitionSpec as P

SPAN = 64
highest = lax.Precision.HIGHEST
reset_level = -30.0


def passed_along(value, axis, steps):
    count = lax.axis_size(axis)
    leading, last = (max(0, -steps), min(count, count - steps))
    return lax.ppermute(value, axis, [(source, source + steps) for source in range(leading, last)])


def rms_gain(values, gain_vec):
    return values * lax.rsqrt(jnp.mean(values * values, -1, keepdims=True) + 1e-06) * gain_vec


def swiglu(joined):
    half_width = joined.shape[-1] // 2
    return jax.nn.silu(joined[..., :half_width]) * joined[..., half_width:]


def short_conv(raw_input, kernel, segment):
    length = raw_input.shape[1]
    tap_count = kernel.shape[0]
    total = raw_input * kernel[tap_count - 1]
    for offset in range(1, tap_count):
        shifted = jnp.pad(raw_input, ((0, 0), (offset, 0), (0, 0)))[:, :length]
        earlier = jnp.pad(segment, ((0, 0), (offset, 0)), constant_values=-1)[:, :length]
        total = (
            total
            + jnp.where((earlier == segment)[..., None], shifted, 0.0)
            * kernel[tap_count - 1 - offset]
        )
    return jax.nn.silu(total)


def delta_rule(queries, key_rows, value_rows, beta_gate, decays, block_len):
    batch_size, head_count, length, key_dim = queries.shape
    value_dim = value_rows.shape[-1]
    block_count = length // block_len

    def to_blocks(array):
        return array.reshape(array.shape[:2] + (block_count, block_len) + array.shape[3:])

    queries = to_blocks(queries)
    key_rows = to_blocks(key_rows)
    value_rows = to_blocks(value_rows)
    beta_gate = to_blocks(beta_gate)
    levels = jnp.cumsum(to_blocks(decays), axis=-1)
    places = jnp.arange(block_len)
    lower_mask = places[:, None] >= places[None, :]
    strict_mask = places[:, None] > places[None, :]
    spread = jnp.exp(jnp.where(lower_mask, levels[..., :, None] - levels[..., None, :], -1e30))
    beta_keys = key_rows * beta_gate[..., None]
    key_inner = jnp.einsum("bhncd,bhnmd->bhncm", beta_keys, key_rows, precision=highest) * spread
    system = jnp.where(strict_mask, key_inner, 0.0)
    right_side = jnp.concatenate(
        [beta_keys * jnp.exp(levels)[..., None], value_rows * beta_gate[..., None]], -1
    )
    solved = lax.linalg.triangular_solve(
        system, right_side, left_side=True, lower=True, unit_diagonal=True
    )
    solved_keys = solved[..., :key_dim]
    solved_values = solved[..., key_dim:]
    scores = jnp.einsum("bhncd,bhnmd->bhncm", queries, key_rows, precision=highest) * spread
    fading = queries * jnp.exp(levels)[..., None]
    final_level = levels[..., -1:]
    carried = key_rows * jnp.exp(final_level - levels)[..., None]

    def advance(memory, pieces):
        fading_part, keys_part, values_part, scores_part, carried_part, final_part = pieces
        update = values_part - jnp.einsum("bhcd,bhde->bhce", keys_part, memory, precision=highest)
        output = jnp.einsum("bhcd,bhde->bhce", fading_part, memory, precision=highest) + jnp.einsum(
            "bhcm,bhme->bhce", scores_part, update, precision=highest
        )
        memory = memory * jnp.exp(final_part)[..., None] + jnp.einsum(
            "bhcd,bhce->bhde", carried_part, update, precision=highest
        )
        return (memory, output)

    pieces = tuple(
        (
            jnp.moveaxis(array, 2, 0)
            for array in (fading, solved_keys, solved_values, scores, carried, final_level)
        )
    )
    initial = jnp.zeros((batch_size, head_count, key_dim, value_dim), queries.dtype)
    _, outputs = lax.scan(advance, initial, pieces)
    return jnp.moveaxis(outputs, 0, 2).reshape(batch_size, head_count, length, value_dim)


def token_mixer(projected, rate_logits, kernel, head_params, out_gain, segment):
    batch_size, length, _ = projected.shape
    head_count = head_params.shape[1]
    value_dim = out_gain.shape[0]
    channels = kernel.shape[1]
    key_width = (channels - head_count * value_dim) // 2
    key_dim = key_width // head_count
    mixed = short_conv(projected[..., :channels], kernel, segment)

    def heads_of(array, size):
        return jnp.moveaxis(array.reshape(batch_size, length, head_count, size), 2, 1)

    queries = heads_of(mixed[..., :key_width], key_dim)
    key_rows = heads_of(mixed[..., key_width : 2 * key_width], key_dim)
    value_rows = heads_of(mixed[..., 2 * key_width :], value_dim)
    queries = (
        queries
        * lax.rsqrt(jnp.sum(queries * queries, -1, keepdims=True) + 1e-06)
        * key_dim ** (-0.5)
    )
    key_rows = key_rows * lax.rsqrt(jnp.sum(key_rows * key_rows, -1, keepdims=True) + 1e-06)
    beta_gate = jax.nn.sigmoid(jnp.moveaxis(rate_logits[..., head_count:], 2, 1))
    decays = -jnp.exp(head_params[0])[:, None] * jax.nn.softplus(
        jnp.moveaxis(rate_logits[..., :head_count], 2, 1) + head_params[1][:, None]
    )
    earlier = jnp.pad(segment, ((0, 0), (1, 0)), constant_values=-1)[:, :length]
    decays = jnp.where((earlier != segment)[:, None, :], reset_level, decays)
    output = delta_rule(queries, key_rows, value_rows, beta_gate, decays, SPAN)
    output = output * lax.rsqrt(jnp.mean(output * output, -1, keepdims=True) + 1e-05) * out_gain
    gating = heads_of(projected[..., channels:], value_dim)
    return jnp.moveaxis(output * jax.nn.silu(gating), 1, 2).reshape(
        batch_size, length, head_count * value_dim
    )


def last_contract(left, right):
    return lax.dot_general(
        left, right, (((2,), (1,)), ((), ())), preferred_element_type=jnp.float32
    )


def layer_forward(entering, segment, weights, small_params):
    norm_gains, proj_weight, rate_weight, out_weight, up_weight, down_weight = weights
    kernel, head_params, out_gain = small_params
    widened = entering.astype(jnp.float32)
    normed_one, norm_one_back = jax.vjp(rms_gain, widened, norm_gains[0].astype(jnp.float32))
    hidden_one = normed_one.astype(jnp.bfloat16)
    projected = jnp.dot(hidden_one, proj_weight, preferred_element_type=jnp.float32)
    rate_logits = jnp.dot(hidden_one, rate_weight, preferred_element_type=jnp.float32)
    mixed_out, mixer_back = jax.vjp(
        partial(token_mixer, segment=segment), projected, rate_logits, kernel, head_params, out_gain
    )
    mixed_half = mixed_out.astype(jnp.bfloat16)
    stream = widened + last_contract(mixed_half, out_weight)
    normed_two, norm_two_back = jax.vjp(rms_gain, stream, norm_gains[1].astype(jnp.float32))
    hidden_two = normed_two.astype(jnp.bfloat16)
    gate_up = jnp.dot(hidden_two, up_weight, preferred_element_type=jnp.float32)
    activated, act_back = jax.vjp(swiglu, gate_up)
    act_half = activated.astype(jnp.bfloat16)
    layer_out = (stream + last_contract(act_half, down_weight)).astype(jnp.bfloat16)
    residuals = (
        norm_one_back,
        hidden_one,
        mixer_back,
        mixed_half,
        norm_two_back,
        hidden_two,
        act_back,
        act_half,
    )
    return (layer_out, residuals)


def layer_backward(cotangent_in, residuals, weights):
    norm_gains, proj_weight, rate_weight, out_weight, up_weight, down_weight = weights
    (
        norm_one_back,
        hidden_one,
        mixer_back,
        mixed_half,
        norm_two_back,
        hidden_two,
        act_back,
        act_half,
    ) = residuals
    dout_half = cotangent_in.astype(jnp.bfloat16)
    (gate_up_grad,) = act_back(jnp.dot(dout_half, down_weight, preferred_element_type=jnp.float32))
    gate_up_cot = gate_up_grad.astype(jnp.bfloat16)
    stream_grad, gain_two = norm_two_back(last_contract(gate_up_cot, up_weight))
    stream_grad = cotangent_in + stream_grad
    branch_cot = stream_grad.astype(jnp.bfloat16)
    proj_grad, rate_grad, kernel_grad, head_grad, out_gain_grad = mixer_back(
        jnp.dot(branch_cot, out_weight, preferred_element_type=jnp.float32)
    )
    proj_cot = proj_grad.astype(jnp.bfloat16)
    rate_cot = rate_grad.astype(jnp.bfloat16)
    hidden_grad = last_contract(proj_cot, proj_weight) + last_contract(rate_cot, rate_weight)
    entry_grad, gain_one = norm_one_back(hidden_grad)
    pairs = (
        hidden_one,
        proj_cot,
        rate_cot,
        mixed_half,
        branch_cot,
        hidden_two,
        gate_up_cot,
        act_half,
        dout_half,
    )
    return (
        stream_grad + entry_grad,
        pairs,
        (kernel_grad, head_grad, out_gain_grad),
        jnp.stack([gain_one, gain_two]),
    )


def weight_terms(pairs, gain_sum, start, count):
    flattened = [member.reshape(-1, member.shape[-1]) for member in pairs]
    (
        hidden_one,
        proj_cot,
        rate_cot,
        mixed_half,
        branch_cot,
        hidden_two,
        gate_up_cot,
        act_half,
        dout_half,
    ) = flattened

    def product(left, right):
        return lax.dot_general(
            left, right, (((0,), (0,)), ((), ())), preferred_element_type=jnp.float32
        )

    return jnp.concatenate(
        [
            product(hidden_one, proj_cot),
            product(hidden_one, rate_cot),
            product(branch_cot, mixed_half),
            product(hidden_two, gate_up_cot),
            product(dout_half, act_half),
            gain_sum.T,
        ],
        1,
    )


def split_term(total, widths):
    pieces = []
    column = 0
    for width in widths:
        pieces.append(total[..., column : column + width])
        column = column + width
    return pieces


def pass_forward(layer_out):
    return passed_along(layer_out, "section", 1)


def pass_backward(entry_grad):
    return passed_along(entry_grad.astype(jnp.bfloat16), "section", -1).astype(entry_grad.dtype)


def shards(
    tokens,
    segments,
    cotangent,
    norm_gains,
    proj_weight,
    rate_weight,
    out_weight,
    up_weight,
    down_weight,
    conv_kernels,
    head_params,
    out_gain,
):
    first_section = lax.axis_index("section") == 0
    weights = (
        lax.all_gather(norm_gains[0], "fsdp", axis=1, tiled=True),
        lax.all_gather(proj_weight[0], "fsdp", axis=0, tiled=True),
        lax.all_gather(rate_weight[0], "fsdp", axis=0, tiled=True),
        lax.all_gather(out_weight[0], "fsdp", axis=0, tiled=True),
        lax.all_gather(up_weight[0], "fsdp", axis=0, tiled=True),
        lax.all_gather(down_weight[0], "fsdp", axis=0, tiled=True),
    )
    small_params = (conv_kernels[0], head_params[0], out_gain[0])
    batches = tokens.shape[0]
    records = []
    results = []
    for forward_step in range(batches + 1):
        ahead_batch = min(forward_step, batches - 1)
        behind = max(forward_step - 1, 0)
        segment = jnp.where(first_section, segments[ahead_batch], segments[behind])
        if forward_step == 0:
            entering = tokens[0]
        else:
            entering = jnp.where(first_section, tokens[ahead_batch], pass_forward(results[-1]))
        produced, residuals = layer_forward(entering, segment, weights, small_params)
        records.append(residuals)
        results.append(produced)
    incoming = []
    kept_pairs = []
    small_list = []
    gain_list = []
    for backward_step in range(batches + 1):
        if backward_step < batches:
            own_cot = cotangent[batches - 1 - backward_step]
        else:
            own_cot = jnp.zeros_like(cotangent[0])
        if backward_step == 0:
            upstream = jnp.zeros_like(own_cot)
        else:
            upstream = pass_backward(incoming[-1])
        dout_full = jnp.where(first_section, upstream, own_cot)
        entry_grad, pairs, small_grads, gains_step = layer_backward(
            dout_full, records[batches - backward_step], weights
        )
        incoming.append(entry_grad)
        kept_pairs.append(pairs)
        small_list.append(small_grads)
        gain_list.append(gains_step)
    pairs_all = tuple((jnp.concatenate([member[i] for member in kept_pairs], 1) for i in range(9)))
    gain_sum = sum(gain_list)
    small_sum = tuple((sum((member[i] for member in small_list)) for i in range(3)))
    section_output = jnp.stack([jnp.where(first_section, results[0], results[1])])[None]
    input_grad = jnp.stack([jnp.where(first_section, incoming[batches], incoming[batches - 1])])[
        None
    ]
    own_rows = proj_weight.shape[1]
    term_of = partial(weight_terms, pairs_all, gain_sum)
    totals = lax.psum_scatter(
        term_of(jnp.int32(0), own_rows * lax.axis_size("fsdp")).astype(jnp.bfloat16),
        "fsdp",
        scatter_dimension=0,
        tiled=True,
    ).astype(jnp.float32)
    totals = lax.psum(totals.astype(jnp.bfloat16), "dp").astype(jnp.float32)
    kernel_grad, head_grad, out_gain_grad = lax.psum(
        (small_sum[0], small_sum[1], small_sum[2]), ("fsdp", "dp")
    )
    widths = [
        proj_weight.shape[2],
        rate_weight.shape[2],
        out_weight.shape[2],
        up_weight.shape[2],
        down_weight.shape[2],
        2,
    ]
    pieces = split_term(totals, widths)
    return (
        section_output,
        input_grad,
        pieces[5].T[None],
        pieces[0][None],
        pieces[1][None],
        pieces[2][None],
        pieces[3][None],
        pieces[4][None],
        kernel_grad[None],
        head_grad[None],
        out_gain_grad[None],
    )


def solution(mesh):
    return jax.shard_map(
        shards,
        mesh=mesh,
        in_specs=(
            P(None, ("fsdp", "dp"), None, None),
            P(None, ("fsdp", "dp"), None),
            P(None, ("fsdp", "dp"), None, None),
            P("section", None, "fsdp"),
            P("section", "fsdp", None),
            P("section", "fsdp", None),
            P("section", "fsdp", None),
            P("section", "fsdp", None),
            P("section", "fsdp", None),
            P("section", None, None),
            P("section", None, None),
            P("section", None),
        ),
        out_specs=(
            P("section", None, ("fsdp", "dp"), None, None),
            P("section", None, ("fsdp", "dp"), None, None),
            P("section", None, "fsdp"),
            P("section", "fsdp", None),
            P("section", "fsdp", None),
            P("section", "fsdp", None),
            P("section", "fsdp", None),
            P("section", "fsdp", None),
            P("section", None, None),
            P("section", None, None),
            P("section", None),
        ),
        check_vma=False,
    )
```

profile of v0, /device:TPU:0, one launch (start us, length us, event | category | flops | bytes accessed | tf_op | source)
XLA Modules:
  0.0 1455.5 jit_solution(11192671535240137623)
XLA Ops:
  10.3 12.7 all-gather
  23.2 13.7 all-gather.1
  41.3 86.5 %all-gather.11.cloned.1.call-done = bf16[1,1024,3072]{2,1,0:T(8,128)(2,1)} async-done(((bf16[1,256,3072]{2,1,0:T(8,128)(2,1)}), bf16[1,1024,3072]{2,1,0:T(8,128)(2,1)}) %all-gather.11.cloned.1.call-update) | async-done | bytes 6291472 | tf_op jit(solution)/shard_map/all_gather | solution.py:280
  141.4 39.3 %custom-call.16 = f32[1,4,2,1,64,64]{4,5,3,2,1,0:T(8,128)S(1)} custom-call(f32[1,4,2,1,64,64]{5,4,3,2,1,0:T(8,128)S(1)} %fusion.409), custom_call_target="InvertDiagBlocksLowerTriangular" | custom-call | tf_op jit(solution)/shard_map/jvp()/triangular_solve/custom-call.1 | solution.py:65
  185.2 7.1 while.96
  201.8 173.0 %all-gather.15.cloned.1.call-done = bf16[1,1024,5632]{2,1,0:T(8,128)(2,1)} async-done(((bf16[1,256,5632]{2,1,0:T(8,128)(2,1)}), bf16[1,1024,5632]{2,1,0:T(8,128)(2,1)}) %all-gather.15.cloned.1.call-update) | async-done | bytes 11534352 | tf_op jit(solution)/shard_map/all_gather | solution.py:283
  374.8 6.0 fusion.166
  382.8 98.3 %all-gather.17.cloned.1.call-done = bf16[1,1024,2816]{2,1,0:T(8,128)(2,1)} async-done(((bf16[1,256,2816]{2,1,0:T(8,128)(2,1)}), bf16[1,1024,2816]{2,1,0:T(8,128)(2,1)}) %all-gather.17.cloned.1.call-update) | async-done | bytes 5767184 | tf_op jit(solution)/shard_map/all_gather | solution.py:284
  481.2 4.6 fusion.242
  515.8 40.7 %custom-call.17 = f32[1,4,2,1,64,64]{4,5,3,2,1,0:T(8,128)} custom-call(f32[1,4,2,1,64,64]{5,4,3,2,1,0:T(8,128)} %fusion.397), custom_call_target="InvertDiagBlocksLowerTriangular" | custom-call | tf_op jit(solution)/shard_map/jvp()/triangular_solve/custom-call.1 | solution.py:65
  576.0 11.5 while.97
  599.8 6.1 fusion.169
  622.0 26.4 %while.98 = (s32[]{:T(128)}, f32[1,4,128,256]{2,3,1,0:T(8,128)S(1)}, f32[2,1,4,64,128]{4,3,0,2,1:T(8,128)}, f32[2,1,4,64,128]{4,3,2,1,0:T(8,128)}, f32[2,1,4,64,...) while((s32[]{:T(128)}, ...), condition=%wide.region_20.23_spmd.clone, body=%wide.region_18.22_spmd.clone.sunk | while | flops 706019328 | bytes 25702096 | solution.py:93
  702.5 4.9 fusion.436
  720.8 19.1 %while.99 = (s32[]{:T(128)}, f32[1,4,128,256]{2,3,1,0:T(8,128)S(1)}, f32[2,1,4,64,128]{4,3,0,2,1:T(8,128)}, f32[2,1,4,64,128]{4,3,2,1,0:T(8,128)}, f32[2,1,4,64,...) while((s32[]{:T(128)}, ...), condition=%wide.region_37.42_spmd.clone, body=%wide.region_35.41_spmd.clone.sunk | while | flops 706019328 | bytes 25701472 | solution.py:93
  762.4 5.6 multiply_reduce_fusion.3
  785.2 4.5 convolution_convert_fusion.2
  796.2 7.3 convolution_convert_fusion
  803.8 5.7 convolution_convert_fusion.1
  809.5 48.0 %concatenate.48 = bf16[1024,12554]{1,0:T(8,128)(2,1)} concatenate(bf16[1024,3072]{1,0:T(8,128)(2,1)} %convolution_convert_fusion.2, bf16[1024,8]{1,0:T(8,128)(2,1)S(1)} %copy.593, bf16[1024,1024]{1,0:T(8,128)(2,1)S(1)} %copy-done.42, bf16[1024,5632]{1,0:T(8,128)(2,1)} %convolution_convert_fusion, bf16[1024,2816]{1,0:T(8,128)(2,1)} %convolution_convert_fusion.1, ...), dimensions={1} | concatenate | bytes 51421184 | tf_op jit(solution)/shard_map/concatenate | solution.py:233
  857.5 427.1 %reduce-scatter.2.cloned.1.call-done = bf16[256,12554]{1,0:T(8,128)(2,1)} async-done(((bf16[1024,12554]{1,0:T(8,128)(2,1)}), bf16[256,12554]{1,0:T(8,128)(2,1)}) %reduce-scatter.2.cloned.1.call-update) | async-done | bytes 6427664 | tf_op jit(solution)/shard_map/reduce_scatter | solution.py:331
  1285.9 5.3 fusion.264
  1291.4 79.9 %all-reduce.51 = (f32[1,4,2048]{2,1,0:T(4,128)}, f32[1,2,4]{2,1,0:T(2,128)}, f32[1,256]{1,0:T(1,128)}) all-reduce(f32[1,4,2048]{2,1,0:T(4,128)S(1)} %add_bitcast_fusion.2, f32[1,2,4]{2,1,0:T(2,128)S(1)} %add_bitcast_fusion.3, f32[1,256]{1,0:T(1,128)S(1)} %bitcast.1621), channel_id=1, replica_groups=mesh['section'=2,'fsdp'=4,'dp'=4] {'fsdp','dp'}, use_global_device_ids=true, to_apply=%region_64.69 | all-reduce | flops 8456 | bytes 67648 | tf_op jit(solution)/shard_map/psum | solution.py:338
  1371.3 62.2 %all-reduce.54.cloned.1.call-done = bf16[256,12554]{1,0:T(8,128)(2,1)} async-done(((bf16[256,12554]{1,0:T(8,128)(2,1)}), bf16[256,12554]{1,0:T(8,128)(2,1)}) %all-reduce.54.cloned.1.call-update) | async-done | bytes 6427664 | tf_op jit(solution)/shard_map/psum | solution.py:337
  (1054 shorter events, 303.8 us)
Async XLA Ops:
  7.2 120.7 %all-gather.11.cloned.1.call-start = ((), (), s32[]{:S(2)}) async-start(), calls=%async_computation.3 | async-start | bytes 7864320 | tf_op jit(solution)/shard_map/all_gather | solution.py:280
  7.9 191.2 %all-gather.13.cloned.1.call-start = ((), (), s32[]{:S(2)}) async-start(), calls=%async_computation.4 | async-start | bytes 2621440 | tf_op jit(solution)/shard_map/all_gather | solution.py:282
  8.7 366.1 %all-gather.15.cloned.1.call-start = ((), (), s32[]{:S(2)}) async-start(), calls=%async_computation.5 | async-start | bytes 14417920 | tf_op jit(solution)/shard_map/all_gather | solution.py:283
  9.5 471.7 %all-gather.17.cloned.1.call-start = ((), (), s32[]{:S(2)}) async-start(), calls=%async_computation.6 | async-start | bytes 7208960 | tf_op jit(solution)/shard_map/all_gather | solution.py:284
  10.0 1274.6 %reduce-scatter.2.cloned.1.call-start = ((), (), s32[]{:S(2)}) async-start(), calls=%async_computation.1 | async-start | bytes 32440320 | tf_op jit(solution)/shard_map/reduce_scatter | solution.py:331
  10.1 130.4 %copy-start.154 = (f32[64,64]{1,0:T(8,128)}, f32[64,64]{1,0:T(8,128)S(1)}, u32[]{:S(2)}) copy-start(f32[64,64]{1,0:T(8,128)S(1)} %get-tuple-element.1668) | copy-start | bytes 49156
  10.1 130.4 %copy-start.161 = (pred[64,64]{1,0:T(8,128)(4,1)}, pred[64,64]{1,0:T(8,128)(4,1)S(1)}, u32[]{:S(2)}) copy-start(pred[64,64]{1,0:T(8,128)(4,1)S(1)} %get-tuple-element.1667) | copy-start | bytes 12292
  10.3 121.5 %copy-start.198 = (pred[128]{0:T(512)(128)(4,1)}, pred[128]{0:T(512)(128)(4,1)S(1)}, u32[]{:S(2)}) copy-start(pred[128]{0:T(512)(128)(4,1)S(1)} %get-tuple-element.1642) | copy-start | bytes 388
  10.3 121.5 %copy-start.202 = (pred[128]{0:T(512)(128)(4,1)}, pred[128]{0:T(512)(128)(4,1)S(1)}, u32[]{:S(2)}) copy-start(pred[128]{0:T(512)(128)(4,1)S(1)} %get-tuple-element.1646) | copy-start | bytes 388
  10.3 121.5 %copy-start.206 = (pred[128]{0:T(512)(128)(4,1)}, pred[128]{0:T(512)(128)(4,1)S(1)}, u32[]{:S(2)}) copy-start(pred[128]{0:T(512)(128)(4,1)S(1)} %get-tuple-element.1647) | copy-start | bytes 388
  23.0 351.8 %copy-start.151 = (f32[1,1,1024]{2,1,0:T(1,128)}, f32[1,1,1024]{2,1,0:T(1,128)S(1)}, u32[]{:S(2)}) copy-start(f32[1,1,1024]{2,1,0:T(1,128)S(1)} %get-tuple-element.1629) | copy-start | bytes 12292
  23.0 468.9 %copy-start.149 = (f32[1,1,1024]{2,1,0:T(1,128)}, f32[1,1,1024]{2,1,0:T(1,128)S(1)}, u32[]{:S(2)}) copy-start(f32[1,1,1024]{2,1,0:T(1,128)S(1)} %get-tuple-element.1630) | copy-start | bytes 12292
  23.2 108.5 %copy-start.239 = (f32[128]{0:T(128)}, f32[128]{0:T(128)S(1)}, u32[]{:S(2)}) copy-start(f32[128]{0:T(128)S(1)} %fusion.515) | copy-start | bytes 1540
  36.9 455.1 %copy-start.159 = (bf16[1,1024,8]{1,2,0:T(8,128)(2,1)}, bf16[1,1024,8]{1,2,0:T(8,128)(2,1)S(1)}, u32[]{:S(2)}) copy-start(bf16[1,1024,8]{1,2,0:T(8,128)(2,1)S(1)} %all-gather.1) | copy-start | bytes 49156
  40.5 97.1 %copy-start.177 = (f32[4,2,64]{2,1,0:T(2,128)}, f32[4,2,64]{2,1,0:T(2,128)S(1)}, u32[]{:S(2)}) copy-start(f32[4,2,64]{2,1,0:T(2,128)S(1)} %get-tuple-element.1632) | copy-start | bytes 6148
  40.5 97.1 %copy-start.181 = (f32[4,2,64]{2,1,0:T(2,128)}, f32[4,2,64]{2,1,0:T(2,128)S(1)}, u32[]{:S(2)}) copy-start(f32[4,2,64]{2,1,0:T(2,128)S(1)} %get-tuple-element.1633) | copy-start | bytes 6148
  40.6 140.2 %copy-start.155 = (f32[4,2,64]{2,1,0:T(2,128)}, f32[4,2,64]{2,1,0:T(2,128)S(1)}, u32[]{:S(2)}) copy-start(f32[4,2,64]{2,1,0:T(2,128)S(1)} %mul.1564) | copy-start | bytes 6148
  201.8 179.1 %copy-start.275 = (f32[128]{0:T(128)}, f32[128]{0:T(128)S(1)}, u32[]{:S(2)}) copy-start(f32[128]{0:T(128)S(1)} %get-tuple-element.1648) | copy-start | bytes 1540
  201.8 279.4 %copy-start.2 = (f32[128,1024]{1,0:T(8,128)}, f32[128,1024]{1,0:T(8,128)S(1)}, u32[]{:S(2)}) copy-start(f32[128,1024]{1,0:T(8,128)S(1)} %get-tuple-element.1649) | copy-start | bytes 1572868
  201.8 179.0 %copy-start.241 = (f32[128]{0:T(128)}, f32[128]{0:T(128)S(1)}, u32[]{:S(2)}) copy-start(f32[128]{0:T(128)S(1)} %fusion.516) | copy-start | bytes 1540
  382.8 103.0 %copy-start.68 = (bf16[1,128,2816]{2,1,0:T(8,128)(2,1)}, bf16[1,128,2816]{2,1,0:T(8,128)(2,1)S(1)}, u32[]{:S(2)}) copy-start(bf16[1,128,2816]{2,1,0:T(8,128)(2,1)S(1)} %multiply_convert_fusion.1) | copy-start | bytes 2162692
  485.8 5.9 collective-permute-start
  697.8 4.6 collective-permute-start.1
  857.5 576.0 %all-reduce.54.cloned.1.call-start = ((), (), s32[]{:S(2)}) async-start(), calls=%async_computation.2 | async-start | bytes 12976128 | tf_op jit(solution)/shard_map/psum | solution.py:337
  (320 other events, 1955.4 us)
Sparse Core Ops, SparseCore 0:
  9.6 118.2 all-gather.10
  129.4 44.0 all-gather.12
  175.1 199.6 all-gather.14
  376.2 104.9 all-gather.16
  857.6 426.9 reduce-scatter.1
  1287.8 145.6 all-reduce.53
where the time goes:
time: 1470 us; the launch traced here: 1460 us
  waiting for transfers between devices  850 us (58%)
  other arithmetic  163 us (11%)
  local copies, waits for them, and re-layouts  161 us (11%)
  matrix products  151 us (10%)
  blocking collectives  106 us (7%)
  between operations  17.9 us (1%)
    reduce_scatter x1, waiting for transfers between devices, shards(): lax.psum_scatter(term_of(jnp.int32(0), own_rows * lax.axis_size('fsdp'))....  427 us
    all_gather x1, waiting for transfers between devices, shards(): lax.all_gather(up_weight[0], 'fsdp', axis=0, tiled=True)  173 us
    all_gather x1, waiting for transfers between devices, shards(): lax.all_gather(down_weight[0], 'fsdp', axis=0, tiled=True)  98.3 us
    all_gather x1, waiting for transfers between devices, shards(): lax.all_gather(proj_weight[0], 'fsdp', axis=0, tiled=True)  86.5 us
    another operation x6, other arithmetic, delta_rule(): lax.linalg.triangular_solve(system, right_side, left_side=True, lower=Tru...  83.3 us
    psum x1, blocking collectives, shards(): lax.psum((small_sum[0], small_sum[1], small_sum[2]), ('fsdp', 'dp'))  79.9 us
    psum x1, waiting for transfers between devices, shards(): totals = lax.psum(totals.astype(jnp.bfloat16), 'dp').astype(jnp.float32)  62.2 us
    concatenate x1, local copies, waits for them, and re-layouts, weight_terms(): jnp.concatenate([product(hidden_one, proj_cot), product(hidden_one, rate_...  48 us
  transfers between devices with their start and end apart: 8, of which 5 were waited for; matrix products, arithmetic and copies ran while one was open for 6% of the time, Pallas kernels for 0%

commit v1 on v0

--- a/solution.py
+++ b/solution.py
@@ -275,9 +275,12 @@
     out_gain,
 ):
     first_section = lax.axis_index("section") == 0
+    gates_attach = lambda a_name, inp: jnp.concatenate(
+        lax.all_to_all(jnp.stack(lax.axis_size(a_name) * [inp], 0), a_name, 0, 0), 0
+    )
     weights = (
         lax.all_gather(norm_gains[0], "fsdp", axis=1, tiled=True),
-        lax.all_gather(proj_weight[0], "fsdp", axis=0, tiled=True),
+        gates_attach("fsdp", proj_weight[0]),
         lax.all_gather(rate_weight[0], "fsdp", axis=0, tiled=True),
         lax.all_gather(out_weight[0], "fsdp", axis=0, tiled=True),
         lax.all_gather(up_weight[0], "fsdp", axis=0, tiled=True),

time: 1470 us -> 1470 us (level)
  waiting for transfers between devices: 850 us -> 583 us
  blocking collectives: 106 us -> 366 us
    all_gather x1, waiting for transfers between devices: 173 us -> 0.02 us  [shards(): lax.all_gather(up_weight[0], 'fsdp', axis=0, tiled=True)]
    all_gather x1, blocking collectives: 12.7 us -> 177 us  [shards(): lax.all_gather(norm_gains[0], 'fsdp', axis=1, tiled=True)]
    all_gather x1, blocking collectives: 13.7 us -> 110 us  [shards(): lax.all_gather(rate_weight[0], 'fsdp', axis=0, tiled=True)]
    all_gather x1 -> x0, waiting for transfers between devices: 86.5 us -> none  [shards(): lax.all_gather(proj_weight[0], 'fsdp', axis=0, tiled=True)]
  transfers between devices with their start and end apart: 8 -> 8, of which waited for: 5 -> 3; matrix products, arithmetic and copies ran while one was open for 6% -> 6% of each run, Pallas kernels for 0% -> 0%
where the time goes in v1:
time: 1470 us; the launch traced here: 1460 us
  waiting for transfers between devices  583 us (40%)
  blocking collectives  366 us (25%)
  local copies, waits for them, and re-layouts  163 us (11%)
  matrix products  162 us (11%)
  other arithmetic  156 us (11%)
  between operations  17.3 us (1%)
    reduce_scatter x1, waiting for transfers between devices, shards(): lax.psum_scatter(term_of(jnp.int32(0), own_rows * lax.axis_size('fsdp'))....  427 us
    all_gather x1, blocking collectives, shards(): lax.all_gather(norm_gains[0], 'fsdp', axis=1, tiled=True)  177 us
    all_gather x1, blocking collectives, shards(): lax.all_gather(rate_weight[0], 'fsdp', axis=0, tiled=True)  110 us
    all_gather x1, waiting for transfers between devices, shards(): lax.all_gather(down_weight[0], 'fsdp', axis=0, tiled=True)  91.7 us
    another operation x6, other arithmetic, delta_rule(): lax.linalg.triangular_solve(system, right_side, left_side=True, lower=Tru...  83.2 us
    psum x1, blocking collectives, shards(): lax.psum((small_sum[0], small_sum[1], small_sum[2]), ('fsdp', 'dp'))  79.9 us
    psum x1, waiting for transfers between devices, shards(): totals = lax.psum(totals.astype(jnp.bfloat16), 'dp').astype(jnp.float32)  62.2 us
    concatenate x1, local copies, waits for them, and re-layouts, weight_terms(): jnp.concatenate([product(hidden_one, proj_cot), product(hidden_one, rate_...  47.9 us
  transfers between devices with their start and end apart: 8, of which 3 were waited for; matrix products, arithmetic and copies ran while one was open for 6% of the time, Pallas kernels for 0%

profile of v1, /device:TPU:0, one launch (start us, length us, event | category | flops | bytes accessed | tf_op | source)
XLA Modules:
  0.0 1460.6 jit_solution(11504457311469812191)
XLA Ops:
  12.1 6.5 all-to-all-start
  19.4 176.6 %all-gather = bf16[1,2,1024]{2,1,0:T(2,128)(2,1)S(1)} all-gather(bf16[1,2,256]{2,1,0:T(2,128)(2,1)S(1)} %copy-done.261), channel_id=2, replica_groups=mesh['section'=2,'fsdp'=4,'dp'=4] {'fsdp'}, dimensions={2}, use_global_device_ids=true | all-gather | bytes 5120 | tf_op jit(solution)/shard_map/all_gather | solution.py:282
  196.0 109.7 %all-gather.1 = bf16[1,1024,8]{1,2,0:T(8,128)(2,1)S(1)} all-gather(bf16[1,256,8]{1,2,0:T(8,128)(2,1)S(1)} %copy-done.254), channel_id=3, replica_groups=mesh['section'=2,'fsdp'=4,'dp'=4] {'fsdp'}, dimensions={1}, use_global_device_ids=true | all-gather | bytes 20480 | tf_op jit(solution)/shard_map/all_gather | solution.py:284
  323.4 39.3 %custom-call.16 = f32[1,4,2,1,64,64]{4,5,3,2,1,0:T(8,128)S(1)} custom-call(f32[1,4,2,1,64,64]{5,4,3,2,1,0:T(8,128)S(1)} %fusion.405), custom_call_target="InvertDiagBlocksLowerTriangular" | custom-call | tf_op jit(solution)/shard_map/jvp()/triangular_solve/custom-call.1 | solution.py:65
  367.2 7.0 while.96
  383.8 7.2 fusion.166
  393.1 91.7 %all-gather.13.cloned.1.call-done = bf16[1,1024,2816]{2,1,0:T(8,128)(2,1)} async-done(((bf16[1,256,2816]{2,1,0:T(8,128)(2,1)}), bf16[1,1024,2816]{2,1,0:T(8,128)(2,1)}) %all-gather.13.cloned.1.call-update) | async-done | bytes 5767184 | tf_op jit(solution)/shard_map/all_gather | solution.py:287
  484.8 4.6 fusion.228
  519.3 40.7 %custom-call.17 = f32[1,4,2,1,64,64]{4,5,3,2,1,0:T(8,128)} custom-call(f32[1,4,2,1,64,64]{5,4,3,2,1,0:T(8,128)} %fusion.393), custom_call_target="InvertDiagBlocksLowerTriangular" | custom-call | tf_op jit(solution)/shard_map/jvp()/triangular_solve/custom-call.1 | solution.py:65
  579.6 11.5 while.97
  603.4 6.1 fusion.169
  625.6 26.3 %while.98 = (s32[]{:T(128)}, f32[1,4,128,256]{2,3,1,0:T(8,128)S(1)}, f32[2,1,4,64,128]{4,3,0,2,1:T(8,128)}, f32[2,1,4,64,128]{4,3,2,1,0:T(8,128)}, f32[2,1,4,64,...) while((s32[]{:T(128)}, ...), condition=%wide.region_20.23_spmd.clone, body=%wide.region_18.22_spmd.clone.sunk | while | flops 706019328 | bytes 25702096 | solution.py:93
  687.0 6.1 fusion.279
  707.0 4.9 fusion.436
  725.3 19.1 %while.99 = (s32[]{:T(128)}, f32[1,4,128,256]{2,3,1,0:T(8,128)S(1)}, f32[2,1,4,64,128]{4,3,0,2,1:T(8,128)}, f32[2,1,4,64,128]{4,3,2,1,0:T(8,128)}, f32[2,1,4,64,...) while((s32[]{:T(128)}, ...), condition=%wide.region_37.42_spmd.clone, body=%wide.region_35.41_spmd.clone.sunk | while | flops 706019328 | bytes 25701472 | solution.py:93
  766.8 5.2 multiply_reduce_fusion.3
  773.8 5.8 fusion.277
  802.0 6.9 convolution_convert_fusion
  809.1 5.9 convolution_convert_fusion.1
  815.0 47.9 %concatenate.48 = bf16[1024,12554]{1,0:T(8,128)(2,1)} concatenate(bf16[1024,3072]{1,0:T(8,128)(2,1)} %convolution_convert_fusion.2, bf16[1024,8]{1,0:T(8,128)(2,1)S(1)} %copy.593, bf16[1024,1024]{1,0:T(8,128)(2,1)S(1)} %copy-done.41, bf16[1024,5632]{1,0:T(8,128)(2,1)} %convolution_convert_fusion, bf16[1024,2816]{1,0:T(8,128)(2,1)} %convolution_convert_fusion.1, ...), dimensions={1} | concatenate | bytes 51421184 | tf_op jit(solution)/shard_map/concatenate | solution.py:233
  863.0 427.1 %reduce-scatter.2.cloned.1.call-done = bf16[256,12554]{1,0:T(8,128)(2,1)} async-done(((bf16[1024,12554]{1,0:T(8,128)(2,1)}), bf16[256,12554]{1,0:T(8,128)(2,1)}) %reduce-scatter.2.cloned.1.call-update) | async-done | bytes 6427664 | tf_op jit(solution)/shard_map/reduce_scatter | solution.py:334
  1291.4 5.3 fusion.250
  1296.9 79.9 %all-reduce.51 = (f32[1,4,2048]{2,1,0:T(4,128)}, f32[1,2,4]{2,1,0:T(2,128)}, f32[1,256]{1,0:T(1,128)}) all-reduce(f32[1,4,2048]{2,1,0:T(4,128)S(1)} %add_bitcast_fusion.2, f32[1,2,4]{2,1,0:T(2,128)S(1)} %add_bitcast_fusion.3, f32[1,256]{1,0:T(1,128)S(1)} %bitcast.1636), channel_id=1, replica_groups=mesh['section'=2,'fsdp'=4,'dp'=4] {'fsdp','dp'}, use_global_device_ids=true, to_apply=%region_64.69 | all-reduce | flops 8456 | bytes 67648 | tf_op jit(solution)/shard_map/psum | solution.py:341
  1376.8 62.2 %all-reduce.54.cloned.1.call-done = bf16[256,12554]{1,0:T(8,128)(2,1)} async-done(((bf16[256,12554]{1,0:T(8,128)(2,1)}), bf16[256,12554]{1,0:T(8,128)(2,1)}) %all-reduce.54.cloned.1.call-update) | async-done | bytes 6427664 | tf_op jit(solution)/shard_map/psum | solution.py:340
  (1028 shorter events, 301.0 us)
Async XLA Ops:
  7.2 373.9 %all-gather.9.cloned.1.call-start = ((), (), s32[]{:S(2)}) async-start(), calls=%async_computation.4 | async-start | bytes 2621440 | tf_op jit(solution)/shard_map/all_gather | solution.py:285
  7.9 375.9 %all-gather.11.cloned.1.call-start = ((), (), s32[]{:S(2)}) async-start(), calls=%async_computation.5 | async-start | bytes 14417920 | tf_op jit(solution)/shard_map/all_gather | solution.py:286
  12.1 183.9 %copy-start.254 = (bf16[1,256,8]{1,2,0:T(8,128)(2,1)S(1)}, bf16[1,256,8]{1,2,0:T(8,128)(2,1)}, u32[]{:S(2)}) copy-start(bf16[1,256,8]{1,2,0:T(8,128)(2,1)} %param.32) | copy-start | bytes 12292
  12.1 293.6 %copy-start.18 = (bf16[1,1,128,1024]{3,2,1,0:T(8,128)(2,1)S(1)}, bf16[1,1,128,1024]{3,2,1,0:T(8,128)(2,1)}, u32[]{:S(2)}) copy-start(bf16[1,1,128,1024]{3,2,1,0:T(8,128)(2,1)} %param.27) | copy-start | bytes 786436
  12.1 298.6 %all-to-all-start = ((bf16[4,256,3072]{2,1,0:T(8,128)(2,1)}), bf16[4,256,3072]{2,1,0:T(8,128)(2,1)}, u32[]{:S(2)}, u32[]{:S(2)}) async-start(bf16[4,256,3072]{2,1,0:T(8,128)(2,1)} %stack.21), calls=%async_computation | async-start | bytes 12582912 | tf_op jit(solution)/shard_map/all_to_all | solution.py:279
  18.6 288.2 %copy-start.255 = (f32[1,2,4]{2,1,0:T(2,128)S(1)}, f32[1,2,4]{2,1,0:T(2,128)}, u32[]{:S(2)}) copy-start(f32[1,2,4]{2,1,0:T(2,128)} %param.37) | copy-start | bytes 100
  18.6 288.2 %copy-start.260 = (s32[1,1,128]{2,1,0:T(1,128)S(1)}, s32[1,1,128]{2,1,0:T(1,128)}, u32[]{:S(2)}) copy-start(s32[1,1,128]{2,1,0:T(1,128)} %param.28) | copy-start | bytes 1540
  18.6 292.0 %copy-start.188 = (f32[1,4,2048]{2,1,0:T(4,128)S(1)}, f32[1,4,2048]{2,1,0:T(4,128)}, u32[]{:S(2)}) copy-start(f32[1,4,2048]{2,1,0:T(4,128)} %param.36) | copy-start | bytes 98308
  18.6 466.2 %all-gather.13.cloned.1.call-start = ((), (), s32[]{:S(2)}) async-start(), calls=%async_computation.6 | async-start | bytes 7208960 | tf_op jit(solution)/shard_map/all_gather | solution.py:287
  19.3 1270.8 %reduce-scatter.2.cloned.1.call-start = ((), (), s32[]{:S(2)}) async-start(), calls=%async_computation.2 | async-start | bytes 32440320 | tf_op jit(solution)/shard_map/reduce_scatter | solution.py:334
  305.7 189.9 %copy-start.154 = (bf16[1,1024,8]{1,2,0:T(8,128)(2,1)}, bf16[1,1024,8]{1,2,0:T(8,128)(2,1)S(1)}, u32[]{:S(2)}) copy-start(bf16[1,1024,8]{1,2,0:T(8,128)(2,1)S(1)} %all-gather.1) | copy-start | bytes 49156
  306.5 77.3 %copy-start.146 = (f32[1,1,1024]{2,1,0:T(1,128)}, f32[1,1,1024]{2,1,0:T(1,128)S(1)}, u32[]{:S(2)}) copy-start(f32[1,1,1024]{2,1,0:T(1,128)S(1)} %get-tuple-element.1629) | copy-start | bytes 12292
  306.5 189.0 %copy-start.144 = (f32[1,1,1024]{2,1,0:T(1,128)}, f32[1,1,1024]{2,1,0:T(1,128)S(1)}, u32[]{:S(2)}) copy-start(f32[1,1,1024]{2,1,0:T(1,128)S(1)} %get-tuple-element.1630) | copy-start | bytes 12292
  309.5 53.3 %copy-start.150 = (f32[4,2,64]{2,1,0:T(2,128)}, f32[4,2,64]{2,1,0:T(2,128)S(1)}, u32[]{:S(2)}) copy-start(f32[4,2,64]{2,1,0:T(2,128)S(1)} %mul.1580) | copy-start | bytes 6148
  320.0 44.0 %copy-start.58 = (f32[1,4,128,128]{3,1,2,0:T(4,128)}, f32[1,4,128,128]{3,1,2,0:T(4,128)S(1)}, u32[]{:S(2)}) copy-start(f32[1,4,128,128]{3,1,2,0:T(4,128)S(1)} %get-tuple-element.1663) | copy-start | bytes 786436
  321.3 42.5 %copy-start.78 = (f32[1,128,4,256]{3,2,1,0:T(4,128)}, f32[1,128,4,256]{3,2,1,0:T(4,128)S(1)}, u32[]{:S(2)}) copy-start(f32[1,128,4,256]{3,2,1,0:T(4,128)S(1)} %reshape.2344) | copy-start | bytes 1572868
  383.7 101.0 %copy-start.2 = (f32[128,1024]{1,0:T(8,128)}, f32[128,1024]{1,0:T(8,128)S(1)}, u32[]{:S(2)}) copy-start(f32[128,1024]{1,0:T(8,128)S(1)} %get-tuple-element.1649) | copy-start | bytes 1572868
  393.0 96.3 %copy-start.67 = (bf16[1,128,2816]{2,1,0:T(8,128)(2,1)}, bf16[1,128,2816]{2,1,0:T(8,128)(2,1)S(1)}, u32[]{:S(2)}) copy-start(bf16[1,128,2816]{2,1,0:T(8,128)(2,1)S(1)} %multiply_convert_fusion.1) | copy-start | bytes 2162692
  489.4 5.9 collective-permute-start
  510.3 64.0 %copy-start = (f32[1,4,128,128]{3,1,2,0:T(4,128)}, f32[1,4,128,128]{3,1,2,0:T(4,128)S(1)}, u32[]{:S(2)}) copy-start(f32[1,4,128,128]{3,1,2,0:T(4,128)S(1)} %bitcast_multiply_fusion.30) | copy-start | bytes 786436
  512.1 49.6 %copy-start.54 = (f32[1,4,128,128]{3,1,2,0:T(4,128)}, f32[1,4,128,128]{3,1,2,0:T(4,128)S(1)}, u32[]{:S(2)}) copy-start(f32[1,4,128,128]{3,1,2,0:T(4,128)S(1)} %fusion.387) | copy-start | bytes 786436
  517.6 44.2 %copy-start.110 = (f32[4,2,64,64]{3,2,1,0:T(8,128)}, f32[4,2,64,64]{3,2,1,0:T(8,128)S(1)}, u32[]{:S(2)}) copy-start(f32[4,2,64,64]{3,2,1,0:T(8,128)S(1)} %fusion.350) | copy-start | bytes 393220
  702.3 4.6 collective-permute-start.1
  863.0 576.0 %all-reduce.54.cloned.1.call-start = ((), (), s32[]{:S(2)}) async-start(), calls=%async_computation.3 | async-start | bytes 12976128 | tf_op jit(solution)/shard_map/psum | solution.py:340
  (308 other events, 1356.2 us)
Sparse Core Ops, SparseCore 0:
  9.6 98.5 all-gather.8
  109.7 267.5 all-gather.10
  378.9 105.8 all-gather.12
  863.1 426.9 reduce-scatter.1
  1293.3 145.6 all-reduce.53
